TPU v7x, 1024 devices: a whole 4x4x32 slice. The times are simulated.
1024 devices in a mesh: context: 32 (over x, y, core), tensor: 32 (over z).
Axes of the slice: x: 4, y: 4, z: 32, core: 2. Of those that a mesh axis runs over, the one named last changes fastest.
Arguments:
- tokens_t: bfloat16 [6144, 8192], P('tensor', 'context'), may hold values from -6 to 6
- qkv_weight: bfloat16 [6144, 24576], P(None, 'tensor'), may hold values from -1.5309311 to 1.5309311, as said below
- prior_state: float32 [64, 128, 128], P('tensor'), may hold values from -192 to 192
- norm_gain: float32 [8192], P('tensor'), may hold values from 0.1 to 1.9
Outputs:
- mixed: bfloat16 [8192, 8192], P('context', 'tensor')
Inputs may be any that keep to these rules, and one draw needn't show every extreme that they name: `qkv_weight`: column h * 3 * 128 + p * 128 + e projects onto feature e of head h, with p = 0, 1, 2 for query, key and value.
All inputs are finite; a program needn't handle non-finite values.
Results may differ from a plain program's by a relative error of at most 0.0034.
Values may be sent and summed in bfloat16 or wider, within the bound.
A program may use at most 32 MiB of HBM per device.

v0:
```python
import jax
import jax.numpy as jnp
from jax import lax
from jax.sharding import PartitionSpec as P

H = 64
HEAD = 128


EPSILON = 1e-06
PRECISE = lax.Precision.HIGHEST


def body(tokens_t, qkv_weight, prior_state, norm_gain):
    tok_rows = tokens_t.shape[1]
    head_count = prior_state.shape[0]
    head_width = prior_state.shape[1]
    projected = lax.dot_general(
        lax.all_gather(tokens_t, "tensor", axis=0, tiled=True),
        qkv_weight,
        (((0,), (0,)), ((), ())),
        preferred_element_type=jnp.float32,
    )
    activated = (
        jax.nn.silu(projected).astype(jnp.bfloat16).reshape(tok_rows, head_count, 3, head_width)
    )
    queries = activated[:, :, 0]
    key_rows = activated[:, :, 1]
    value_rows = activated[:, :, 2]
    group_state = jnp.einsum(
        "thd,the->hde", key_rows, value_rows, preferred_element_type=jnp.float32
    )
    my_index = lax.axis_index("context")
    block_part = lax.all_gather(group_state[None], "context", axis=0, tiled=True)
    positions = jnp.arange(block_part.shape[0])
    keep_rows = (positions < my_index).astype(jnp.float32)
    earlier = jnp.sum(keep_rows[:, None, None, None] * block_part, axis=0)
    carried = prior_state + earlier
    causal = jnp.arange(tok_rows)[:, None] >= jnp.arange(tok_rows)[None, :]
    scores = jnp.einsum("thd,shd->hts", queries, key_rows, preferred_element_type=jnp.float32)
    scores = jnp.where(causal[None], scores, 0.0).astype(jnp.bfloat16)
    within_term = jnp.einsum("hts,shd->thd", scores, value_rows, preferred_element_type=jnp.float32)
    carried_term = jnp.einsum(
        "thd,hde->the", queries.astype(jnp.float32), carried, precision=PRECISE
    )
    attended = (within_term + carried_term).reshape(tok_rows, head_count * head_width)
    square_sum = lax.psum(jnp.sum(attended * attended, axis=1), "tensor")
    inverse_rms = lax.rsqrt(square_sum / (H * HEAD) + EPSILON)
    return (attended * inverse_rms[:, None] * norm_gain[None, :]).astype(jnp.bfloat16)


def solution(mesh):
    in_specs = (P("tensor", "context"), P(None, "tensor"), P("tensor", None, None), P("tensor"))
    out_specs = P("context", "tensor")
    return jax.shard_map(body, mesh=mesh, in_specs=in_specs, out_specs=out_specs, check_vma=False)
```

profile of v0, /device:TPU:2, one launch (start us, length us, event | category | flops | bytes accessed | tf_op | source)
XLA Modules:
  0.0 308.8 jit_solution(7877230991956601666)
XLA Ops:
  6.5 0.0 all-gather.4.cloned.1.call-start
  6.5 0.7 all-gather.4.cloned.1.call-update
  7.3 0.0 all-gather.6.cloned.1.call-start
  7.3 151.0 %all-gather.4.cloned.1.call-done = bf16[6144,256]{1,0:T(8,128)(2,1)} async-done(((bf16[192,256]{1,0:T(8,128)(2,1)}), bf16[6144,256]{1,0:T(8,128)(2,1)}) %all-gather.4.cloned.1.call-update) | async-done | bytes 3145744 | tf_op jit(solution)/shard_map/all_gather | solution.py:19
  158.3 7.3 %multiply_convert_fusion = bf16[256,768]{1,0:T(8,128)(2,1)S(1)} fusion(bf16[6144,256]{1,0:T(8,128)(2,1)} %all-gather.4.cloned.1.call-done, bf16[6144,768]{1,0:T(8,128)(2,1)} %param.5), kind=kOutput, calls=%fused_computation.5 | convolution fusion | flops 2416902144 | bytes 12976128 | tf_op jit(solution)/shard_map/dot_general | solution.py:18
  165.7 0.0 copy-start
  165.7 0.0 copy-start.1
  165.7 0.2 copy.18
  165.9 0.8 fusion.6
  166.7 0.0 all-gather.6.cloned.1.call-update
  166.8 0.4 fusion.1
  167.2 72.0 %all-gather.6.cloned.1.call-done = f32[64,128,128]{2,1,0:T(8,128)} async-done(((f32[2,128,128]{2,1,0:T(8,128)}), f32[64,128,128]{2,1,0:T(8,128)}) %all-gather.6.cloned.1.call-update) | async-done | bytes 4194320 | tf_op jit(solution)/shard_map/all_gather | solution.py:34
  239.2 2.6 multiply_reduce_fusion
  241.8 0.0 copy-done
  241.8 0.4 fusion.2
  242.2 58.9 %psum.7 = f32[256]{0:T(256)S(1)} all-reduce(f32[256]{0:T(256)S(1)} %get-tuple-element.5), channel_id=1, replica_groups=mesh['context'=32,'tensor'=32] {'tensor'}, use_global_device_ids=true, to_apply=%region_2.3 | all-reduce | flops 256 | bytes 2048 | tf_op jit(solution)/shard_map/psum | solution.py:47
  301.1 0.1 copy.25
  301.2 0.0 copy-done.1
  301.2 0.8 multiply_convert_fusion.1
  (3 shorter events, 0.0 us)
Async XLA Ops:
  6.5 151.8 %all-gather.4.cloned.1.call-start = ((), (), s32[]{:S(2)}) async-start(), calls=%async_computation | async-start | bytes 3244032 | tf_op jit(solution)/shard_map/all_gather | solution.py:19
  7.3 231.9 %all-gather.6.cloned.1.call-start = ((), (), s32[]{:S(2)}) async-start(), calls=%async_computation.1 | async-start | bytes 4325376 | tf_op jit(solution)/shard_map/all_gather | solution.py:34
  165.7 76.1 %copy-start = (f32[2,128,128]{2,1,0:T(8,128)S(1)}, f32[2,128,128]{2,1,0:T(8,128)}, u32[]{:S(2)}) copy-start(f32[2,128,128]{2,1,0:T(8,128)} %param.6) | copy-start | bytes 393220
  165.7 135.5 %copy-start.1 = (f32[256]{0:T(256)S(1)}, f32[256]{0:T(256)}, u32[]{:S(2)}) copy-start(f32[256]{0:T(256)} %param.7) | copy-start | bytes 3076
Sparse Core Ops, SparseCore 0:
  10.0 148.2 all-gather.3
  166.8 72.2 all-gather.5
where the time goes:
time: 309 us
  waiting for transfers between devices  224 us (72%)
  blocking collectives  58.9 us (19%)
  between operations  13.5 us (4%)
  matrix products  8.96 us (3%)
  other arithmetic  3.4 us (1%)
    all_gather x1, waiting for transfers between devices, body(): lax.all_gather(tokens_t, 'tensor', axis=0, tiled=True)  151 us
    all_gather x1, waiting for transfers between devices, body(): lax.all_gather(group_state[None], 'context', axis=0, tiled=True)  72 us
    psum x1, blocking collectives, body(): square_sum = lax.psum(jnp.sum(attended * attended, axis=1), 'tensor')  58.9 us
    dot_general x1, matrix products, body(): lax.dot_general(lax.all_gather(tokens_t, 'tensor', axis=0, tiled=True), q...  7.34 us
  transfers between devices with their start and end apart: 2, of which 2 were waited for; matrix products, arithmetic and copies ran while one was open for 0% of the time, Pallas kernels for 0%

commit v1 on v0

v1 whole, which is shorter than its diff:
```python
import functools

import jax
import jax.numpy as jnp
from jax import lax
from jax.experimental import pallas as pl
from jax.experimental.pallas import tpu as pltpu
from jax.sharding import PartitionSpec as P

HEAD = 128
EPSILON = 1e-06
CHUNKS = 4
X_CHIPS = 4
F32 = jnp.float32
BF16 = jnp.bfloat16
MESH = pl.DeviceIdType.MESH


def silu(u):
    return u / (1.0 + jnp.exp(-u))


def wait_bytes(ref, sem):
    pltpu.make_async_copy(ref, ref, sem).wait()


def kernel(
    nc, nx, nz, width,
    x_ref, w_ref, prior_ref, gain_ref, out_ref,
    xbuf, wbuf, prior, gain, acc, sbuf, gath, pref, carr, ssq,
    send, recv, local, send1, recv1, send2, recv2, send3, recv3,
):
    ny = nc // (2 * nx)
    half = nz // 2
    rows = xbuf.shape[1]
    piece = rows // CHUNKS
    heads = prior_ref.shape[0]
    c = lax.axis_index("context")
    z = lax.axis_index("tensor")
    neighbour = (lax.rem(z + 1, nz), lax.rem(z + nz - 1, nz))

    px, py, pk = c // (2 * ny), lax.rem(c // 2, ny), lax.rem(c, 2)
    offsets = [(dx, dy, dk) for dx in range(nx) for dy in range(ny) for dk in range(2)]
    offsets = sorted(offsets[1:], key=lambda o: -(min(o[0], nx - o[0]) + min(o[1], ny - o[1])))

    def peer(offset):
        dx, dy, dk = offset
        return (lax.rem(px + dx, nx) * ny + lax.rem(py + dy, ny)) * 2 + lax.rem(pk + dk, 2)

    own = pltpu.make_async_copy(x_ref, xbuf.at[z], local.at[0])
    weights = pltpu.make_async_copy(w_ref, wbuf, local.at[1])
    prior_in = pltpu.make_async_copy(prior_ref, prior, local.at[2])
    gain_in = pltpu.make_async_copy(gain_ref, gain, local.at[3])

    barrier = pltpu.get_barrier_semaphore()
    for d in range(2):
        pl.semaphore_signal(
            barrier, inc=1, device_id={"tensor": neighbour[d]}, device_id_type=MESH
        )
    for offset in offsets:
        pl.semaphore_signal(
            barrier, inc=1, device_id={"context": peer(offset)}, device_id_type=MESH
        )
    own.start()
    weights.start()
    prior_in.start()
    gain_in.start()
    pl.semaphore_wait(barrier, len(offsets) + 2)

    def source(d, s):
        return lax.rem(z + (nz - s if d == 0 else s), nz)

    def part(j):
        return pl.ds(j * piece, piece)

    def forward(d, s, j, src):
        at = source(d, s)
        pltpu.make_async_remote_copy(
            src_ref=src,
            dst_ref=xbuf.at[at, part(j)],
            send_sem=send.at[d, s, j],
            recv_sem=recv.at[d, s + 1, j],
            device_id={"tensor": neighbour[d]},
            device_id_type=MESH,
        ).start()

    def arrived(d, s, j):
        wait_bytes(xbuf.at[source(d, s), part(j)], recv.at[d, s, j])

    def project(at):
        return lax.dot_general(
            xbuf[at], wbuf[at], (((0,), (0,)), ((), ())), preferred_element_type=F32
        )

    for j in range(CHUNKS):
        for d in range(2):
            forward(d, 0, j, x_ref.at[part(j)])

    def relay(s, final):
        for j in range(CHUNKS):
            for d in range(2):
                arrived(d, s, j)
                if not final or (j < CHUNKS // 2) == (d == 0):
                    forward(d, s, j, xbuf.at[source(d, s), part(j)])

    relay(1, False)
    own.wait()
    weights.wait()
    acc[...] = project(z)

    @pl.loop(2, half - 1)
    def _(s):
        relay(s, False)
        acc[...] += project(source(0, s - 1)) + project(source(1, s - 1))

    relay(half - 1, True)
    for s in (half - 2, half - 1):
        acc[...] += project(source(0, s)) + project(source(1, s))
    for j in range(CHUNKS):
        arrived(0 if j < CHUNKS // 2 else 1, half, j)
    acc[...] += project(source(0, half))

    keys, values = [], []
    per = nc // heads
    for h in range(heads):
        base = h * 3 * HEAD
        keys.append(silu(acc[:, base + HEAD : base + 2 * HEAD]).astype(BF16))
        values.append(silu(acc[:, base + 2 * HEAD : base + 3 * HEAD]).astype(BF16))
        state = lax.dot_general(
            keys[h], values[h], (((0,), (0,)), ((), ())), preferred_element_type=F32
        )
        sbuf[h * per : (h + 1) * per] = state.reshape(per, HEAD // per, HEAD)

    def exchange(src, dst, send_sem, recv_sem):
        for offset in offsets:
            to = peer(offset)
            pltpu.make_async_remote_copy(
                src_ref=src.at[to],
                dst_ref=dst.at[c],
                send_sem=send_sem,
                recv_sem=recv_sem,
                device_id={"context": to},
                device_id_type=MESH,
            ).start()

    others = pl.ds(0, nc - 1)
    exchange(sbuf, gath, send1, recv1)
    gath[c] = sbuf[c]

    queries, within = [], []
    tokens = acc.shape[0]
    causal = lax.broadcasted_iota(jnp.int32, (tokens, tokens), 0) >= lax.broadcasted_iota(
        jnp.int32, (tokens, tokens), 1
    )
    for h in range(heads):
        base = h * 3 * HEAD
        queries.append(silu(acc[:, base : base + HEAD]).astype(BF16))
        scores = lax.dot_general(
            queries[h], keys[h], (((1,), (1,)), ((), ())), preferred_element_type=F32
        )
        scores = jnp.where(causal, scores, 0.0).astype(BF16)
        within.append(jnp.dot(scores, values[h], preferred_element_type=F32))

    wait_bytes(gath.at[others], recv1)
    running = jnp.zeros(gath.shape[1:], F32)
    for i in range(nc):
        pref[i] = running
        running = running + gath[i]
    exchange(pref, carr, send2, recv2)
    carr[c] = pref[c]
    prior_in.wait()
    gain_in.wait()
    wait_bytes(carr.at[others], recv2)

    attended = []
    for h in range(heads):
        carried = prior[h] + carr[h * per : (h + 1) * per].reshape(HEAD, HEAD)
        high = carried.astype(BF16)
        low = (carried - high.astype(F32)).astype(BF16)
        across = jnp.dot(queries[h], high, preferred_element_type=F32)
        across += jnp.dot(queries[h], low, preferred_element_type=F32)
        attended.append(within[h] + across)
    squares = attended[0] * attended[0]
    for h in range(1, heads):
        squares += attended[h] * attended[h]
    ssq[z] = jnp.sum(squares.T, axis=0, keepdims=True)

    def tell(to):
        pltpu.make_async_remote_copy(
            src_ref=ssq.at[z],
            dst_ref=ssq.at[z],
            send_sem=send3,
            recv_sem=recv3,
            device_id={"tensor": to},
            device_id_type=MESH,
        ).start()

    tell(source(1, half))

    @pl.loop(1, half)
    def _(i):
        tell(source(0, half - i))
        tell(source(1, half - i))

    peers = pl.ds(0, nz - 1)
    wait_bytes(ssq.at[peers], recv3)
    total = jnp.sum(ssq[...], axis=0)
    inverse = lax.rsqrt(total / width + EPSILON)
    column = jnp.broadcast_to(inverse, (HEAD, tokens)).T
    for h in range(heads):
        span = slice(h * HEAD, (h + 1) * HEAD)
        out_ref[:, span] = (attended[h] * column * gain[:, span]).astype(out_ref.dtype)

    wait_bytes(sbuf.at[others], send1)
    wait_bytes(pref.at[others], send2)
    wait_bytes(ssq.at[peers], send3)

    @pl.loop(0, half - 1)
    def _(s):
        for j in range(CHUNKS):
            for d in range(2):
                wait_bytes(xbuf.at[z, part(j)], send.at[d, s, j])

    for j in range(CHUNKS):
        wait_bytes(xbuf.at[z, part(j)], send.at[0 if j < CHUNKS // 2 else 1, half - 1, j])


def solution(mesh):
    nc, nz = mesh.shape["context"], mesh.shape["tensor"]
    nx = X_CHIPS if nc == 2 * X_CHIPS * X_CHIPS else 2

    def body(tokens_t, qkv_weight, prior_state, norm_gain):
        rows, tokens = tokens_t.shape
        heads = prior_state.shape[0]
        columns = qkv_weight.shape[1]
        tile = heads * HEAD // nc
        width = norm_gain.shape[0] * nz
        any_space = pl.BlockSpec(memory_space=pl.ANY)
        return pl.pallas_call(
            functools.partial(kernel, nc, nx, nz, width),
            out_shape=jax.ShapeDtypeStruct((tokens, heads * HEAD), BF16),
            in_specs=[any_space] * 4,
            out_specs=pl.BlockSpec(memory_space=pltpu.VMEM),
            scratch_shapes=[
                pltpu.VMEM((nz, rows, tokens), BF16),
                pltpu.VMEM((nz, rows, columns), BF16),
                pltpu.VMEM((heads, HEAD, HEAD), F32),
                pltpu.VMEM((1, heads * HEAD), F32),
                pltpu.VMEM((tokens, columns), F32),
                pltpu.VMEM((nc, tile, HEAD), F32),
                pltpu.VMEM((nc, tile, HEAD), F32),
                pltpu.VMEM((nc, tile, HEAD), F32),
                pltpu.VMEM((nc, tile, HEAD), F32),
                pltpu.VMEM((nz, 1, tokens), F32),
                pltpu.SemaphoreType.DMA((2, nz // 2, CHUNKS)),
                pltpu.SemaphoreType.DMA((2, nz // 2 + 1, CHUNKS)),
                pltpu.SemaphoreType.DMA((4,)),
            ]
            + [pltpu.SemaphoreType.DMA] * 6,
            compiler_params=pltpu.CompilerParams(
                collective_id=0, has_side_effects=True, vmem_limit_bytes=48 << 20
            ),
        )(
            tokens_t,
            qkv_weight.reshape(nz, rows, columns),
            prior_state,
            norm_gain.reshape(1, -1),
        )

    in_specs = (P("tensor", "context"), P(None, "tensor"), P("tensor", None, None), P("tensor"))
    out_specs = P("context", "tensor")
    return jax.shard_map(body, mesh=mesh, in_specs=in_specs, out_specs=out_specs, check_vma=False)
```

time: 309 us -> 105 us (0.34)
  the two profiles are of different devices: /device:TPU:2 before, /device:TPU:1 now
where the time goes in v1:
time: 105 us
  Pallas kernels  102 us (97%)
  local copies, waits for them, and re-layouts  3.13 us (3%)
    pallas_call x1, Pallas kernels, body(): pl.pallas_call(functools.partial(kernel, nc, nx, nz, width), out_shape=ja...  102 us
    unnamed x7, local copies, waits for them, and re-layouts  3.13 us

profile of v1, /device:TPU:1, one launch (start us, length us, event | category | flops | bytes accessed | tf_op | source)
XLA Modules:
  0.0 104.9 jit_solution(16701908405170281462)
XLA Ops:
  0.0 0.0 copy-start
  0.0 0.9 copy-done
  0.9 0.0 copy-start.1
  0.9 0.9 copy-done.1
  1.8 0.0 copy-start.2
  1.8 0.7 copy-done.2
  2.5 101.7 %shard_map.46 = bf16[256,256]{1,0:T(8,128)(2,1)S(1)} custom-call(bf16[192,256]{1,0:T(8,128)(2,1)S(1)} %copy-done.1, bf16[32,192,768]{2,1,0:T(8,128)(2,1)} %bitcast.3, f32[2,128,128]{2,1,0:T(8,128)S(1)} %copy-done, f32[1,256]{1,0:T(1,128)S(1)} %bitcast.2), custom_call_target="tpu_custom_call" | custom-call | tf_op jit(solution)/shard_map/pallas_call | solution.py:239
  104.2 0.7 copy.6
Async XLA Ops:
  0.0 0.9 copy-start
  0.9 0.9 copy-start.1
  1.8 0.7 copy-start.2

commit v2 on v1

--- a/solution.py
+++ b/solution.py
@@ -28,7 +28,7 @@
     nc, nx, nz, width,
     x_ref, w_ref, prior_ref, gain_ref, out_ref,
     xbuf, wbuf, prior, gain, acc, sbuf, gath, pref, carr, ssq,
-    send, recv, local, send1, recv1, send2, recv2, send3, recv3,
+    send, recv, local, send1, recv1, send2, recv2, send3, recv3, entered,
 ):
     ny = nc // (2 * nx)
     half = nz // 2
@@ -40,12 +40,16 @@
     neighbour = (lax.rem(z + 1, nz), lax.rem(z + nz - 1, nz))
 
     px, py, pk = c // (2 * ny), lax.rem(c // 2, ny), lax.rem(c, 2)
-    offsets = [(dx, dy, dk) for dx in range(nx) for dy in range(ny) for dk in range(2)]
-    offsets = sorted(offsets[1:], key=lambda o: -(min(o[0], nx - o[0]) + min(o[1], ny - o[1])))
-
-    def peer(offset):
-        dx, dy, dk = offset
-        return (lax.rem(px + dx, nx) * ny + lax.rem(py + dy, ny)) * 2 + lax.rem(pk + dk, 2)
+
+    def at_chip(x, y, k):
+        return (x * ny + y) * 2 + k
+
+    sibling = at_chip(px, py, 1 - pk)
+    along_y = [at_chip(px, lax.rem(py + d, ny), pk) for d in (1, ny - 1)]
+    along_x = [at_chip(lax.rem(px + d, nx), py, pk) for d in (1, nx - 1)]
+
+    def signal(sem, to):
+        pl.semaphore_signal(sem, inc=1, device_id={"context": to}, device_id_type=MESH)
 
     own = pltpu.make_async_copy(x_ref, xbuf.at[z], local.at[0])
     weights = pltpu.make_async_copy(w_ref, wbuf, local.at[1])
@@ -57,15 +61,13 @@
         pl.semaphore_signal(
             barrier, inc=1, device_id={"tensor": neighbour[d]}, device_id_type=MESH
         )
-    for offset in offsets:
-        pl.semaphore_signal(
-            barrier, inc=1, device_id={"context": peer(offset)}, device_id_type=MESH
-        )
+    for to in [sibling] + along_y + along_x:
+        signal(barrier, to)
     own.start()
     weights.start()
     prior_in.start()
     gain_in.start()
-    pl.semaphore_wait(barrier, len(offsets) + 2)
+    pl.semaphore_wait(barrier, 7)
 
     def source(d, s):
         return lax.rem(z + (nz - s if d == 0 else s), nz)
@@ -103,48 +105,73 @@
                 if not final or (j < CHUNKS // 2) == (d == 0):
                     forward(d, s, j, xbuf.at[source(d, s), part(j)])
 
+    for to in along_y:
+        signal(entered.at[0], to)
     relay(1, False)
+    pl.semaphore_wait(entered.at[0], 2)
+    for to in along_x:
+        signal(entered.at[1], to)
+    relay(2, False)
     own.wait()
     weights.wait()
-    acc[...] = project(z)
-
-    @pl.loop(2, half - 1)
+    acc[...] = project(z) + project(source(0, 1)) + project(source(1, 1))
+
+    @pl.loop(3, half - 1)
     def _(s):
         relay(s, False)
         acc[...] += project(source(0, s - 1)) + project(source(1, s - 1))
 
+    pl.semaphore_wait(entered.at[1], 2)
+    for to in along_x:
+        signal(entered.at[2], to)
     relay(half - 1, True)
     for s in (half - 2, half - 1):
         acc[...] += project(source(0, s)) + project(source(1, s))
+    pl.semaphore_wait(entered.at[2], 2)
+    signal(entered.at[3], sibling)
+    last = source(0, half)
     for j in range(CHUNKS):
         arrived(0 if j < CHUNKS // 2 else 1, half, j)
-    acc[...] += project(source(0, half))
-
+
+    def activated(begin, count):
+        span = pl.ds(begin * HEAD, count * HEAD)
+        u = acc[:, span] + lax.dot_general(
+            xbuf[last], wbuf[last, :, span], (((0,), (0,)), ((), ())), preferred_element_type=F32
+        )
+        return silu(u).astype(BF16)
+
+    def exchange(h, src, dst, send_sem, recv_sem):
+        for dy in sorted(range(ny), key=lambda d: -min(d, ny - d)):
+            for x in range(h * nx // heads, (h + 1) * nx // heads):
+                for dk in (1, 0):
+                    to = at_chip(x, lax.rem(py + dy, ny), pk if dk == 0 else 1 - pk)
+                    copy = pltpu.make_async_remote_copy(
+                        src_ref=src.at[to],
+                        dst_ref=dst.at[c],
+                        send_sem=send_sem,
+                        recv_sem=recv_sem,
+                        device_id={"context": to},
+                        device_id_type=MESH,
+                    )
+                    if dy or dk:
+                        copy.start()
+                    else:
+                        pl.when(px != x)(copy.start)
+
+    others = pl.ds(0, nc - 1)
     keys, values = [], []
     per = nc // heads
     for h in range(heads):
-        base = h * 3 * HEAD
-        keys.append(silu(acc[:, base + HEAD : base + 2 * HEAD]).astype(BF16))
-        values.append(silu(acc[:, base + 2 * HEAD : base + 3 * HEAD]).astype(BF16))
+        pair = activated(3 * h + 1, 2)
+        keys.append(pair[:, :HEAD])
+        values.append(pair[:, HEAD:])
         state = lax.dot_general(
             keys[h], values[h], (((0,), (0,)), ((), ())), preferred_element_type=F32
         )
         sbuf[h * per : (h + 1) * per] = state.reshape(per, HEAD // per, HEAD)
-
-    def exchange(src, dst, send_sem, recv_sem):
-        for offset in offsets:
-            to = peer(offset)
-            pltpu.make_async_remote_copy(
-                src_ref=src.at[to],
-                dst_ref=dst.at[c],
-                send_sem=send_sem,
-                recv_sem=recv_sem,
-                device_id={"context": to},
-                device_id_type=MESH,
-            ).start()
-
-    others = pl.ds(0, nc - 1)
-    exchange(sbuf, gath, send1, recv1)
+        if h == 0:
+            pl.semaphore_wait(entered.at[3], 1)
+        exchange(h, sbuf, gath, send1, recv1)
     gath[c] = sbuf[c]
 
     queries, within = [], []
@@ -153,8 +180,7 @@
         jnp.int32, (tokens, tokens), 1
     )
     for h in range(heads):
-        base = h * 3 * HEAD
-        queries.append(silu(acc[:, base : base + HEAD]).astype(BF16))
+        queries.append(activated(3 * h, 1))
         scores = lax.dot_general(
             queries[h], keys[h], (((1,), (1,)), ((), ())), preferred_element_type=F32
         )
@@ -166,7 +192,8 @@
     for i in range(nc):
         pref[i] = running
         running = running + gath[i]
-    exchange(pref, carr, send2, recv2)
+    for h in range(heads):
+        exchange(h, pref, carr, send2, recv2)
     carr[c] = pref[c]
     prior_in.wait()
     gain_in.wait()
@@ -256,9 +283,10 @@
                 pltpu.SemaphoreType.DMA((2, nz // 2 + 1, CHUNKS)),
                 pltpu.SemaphoreType.DMA((4,)),
             ]
-            + [pltpu.SemaphoreType.DMA] * 6,
+            + [pltpu.SemaphoreType.DMA] * 6
+            + [pltpu.SemaphoreType.REGULAR((4,))],
             compiler_params=pltpu.CompilerParams(
-                collective_id=0, has_side_effects=True, vmem_limit_bytes=48 << 20
+                collective_id=0, has_side_effects=True, vmem_limit_bytes=60 * 1024 * 1024
             ),
         )(
             tokens_t,

time: 105 us -> 102 us (0.971)
  Pallas kernels: 102 us -> 100 us
  local copies, waits for them, and re-layouts: 3.13 us -> 1.57 us
    unnamed x7 -> x1, local copies, waits for them, and re-layouts: 3.13 us -> 1.57 us
    pallas_call x1, Pallas kernels: 102 us -> 100 us  [body(): pl.pallas_call(functools.partial(kernel, nc, nx, nz, width), out_shape=ja...]
where the time goes in v2:
time: 102 us
  Pallas kernels  100 us (98%)
  local copies, waits for them, and re-layouts  1.57 us (2%)
    pallas_call x1, Pallas kernels, body(): pl.pallas_call(functools.partial(kernel, nc, nx, nz, width), out_shape=ja...  100 us

profile of v2, /device:TPU:1, one launch (start us, length us, event | category | flops | bytes accessed | tf_op | source)
XLA Modules:
  0.0 102.0 jit_solution(5644136266005334330)
XLA Ops:
  0.0 100.4 %shard_map.46 = bf16[256,256]{1,0:T(8,128)(2,1)} custom-call(bf16[192,256]{1,0:T(8,128)(2,1)} %x_ref.1, bf16[32,192,768]{2,1,0:T(8,128)(2,1)} %bitcast.2, f32[2,128,128]{2,1,0:T(8,128)} %prior_ref.1, f32[1,256]{1,0:T(1,128)} %bitcast.3), custom_call_target="tpu_custom_call" | custom-call | tf_op jit(solution)/shard_map/pallas_call | solution.py:266
  100.5 1.6 %copy.6 = bf16[256,256]{1,0:T(8,128)(2,1)} copy(bf16[256,256]{1,0:T(8,128)(2,1)} %shard_map.46) | data formatting | bytes 262144

commit v3 on v2

--- a/solution.py
+++ b/solution.py
@@ -37,7 +37,6 @@
     heads = prior_ref.shape[0]
     c = lax.axis_index("context")
     z = lax.axis_index("tensor")
-    neighbour = (lax.rem(z + 1, nz), lax.rem(z + nz - 1, nz))
 
     px, py, pk = c // (2 * ny), lax.rem(c // 2, ny), lax.rem(c, 2)
 
@@ -57,9 +56,9 @@
     gain_in = pltpu.make_async_copy(gain_ref, gain, local.at[3])
 
     barrier = pltpu.get_barrier_semaphore()
-    for d in range(2):
+    for away in (1, 2, nz - 2, nz - 1):
         pl.semaphore_signal(
-            barrier, inc=1, device_id={"tensor": neighbour[d]}, device_id_type=MESH
+            barrier, inc=1, device_id={"tensor": lax.rem(z + away, nz)}, device_id_type=MESH
         )
     for to in [sibling] + along_y + along_x:
         signal(barrier, to)
@@ -67,7 +66,7 @@
     weights.start()
     prior_in.start()
     gain_in.start()
-    pl.semaphore_wait(barrier, 7)
+    pl.semaphore_wait(barrier, 9)
 
     def source(d, s):
         return lax.rem(z + (nz - s if d == 0 else s), nz)
@@ -75,14 +74,14 @@
     def part(j):
         return pl.ds(j * piece, piece)
 
-    def forward(d, s, j, src):
+    def forward(d, s, a, j, src):
         at = source(d, s)
         pltpu.make_async_remote_copy(
             src_ref=src,
             dst_ref=xbuf.at[at, part(j)],
-            send_sem=send.at[d, s, j],
-            recv_sem=recv.at[d, s + 1, j],
-            device_id={"tensor": neighbour[d]},
+            send_sem=send.at[d, a - 1, j],
+            recv_sem=recv.at[d, a, j],
+            device_id={"tensor": source(1 - d, a - s)},
             device_id_type=MESH,
         ).start()
 
@@ -94,44 +93,84 @@
             xbuf[at], wbuf[at], (((0,), (0,)), ((), ())), preferred_element_type=F32
         )
 
-    for j in range(CHUNKS):
-        for d in range(2):
-            forward(d, 0, j, x_ref.at[part(j)])
-
-    def relay(s, final):
-        for j in range(CHUNKS):
-            for d in range(2):
-                arrived(d, s, j)
-                if not final or (j < CHUNKS // 2) == (d == 0):
-                    forward(d, s, j, xbuf.at[source(d, s), part(j)])
-
-    for to in along_y:
-        signal(entered.at[0], to)
-    relay(1, False)
-    pl.semaphore_wait(entered.at[0], 2)
-    for to in along_x:
-        signal(entered.at[1], to)
-    relay(2, False)
-    own.wait()
-    weights.wait()
-    acc[...] = project(z) + project(source(0, 1)) + project(source(1, 1))
-
-    @pl.loop(3, half - 1)
-    def _(s):
-        relay(s, False)
-        acc[...] += project(source(0, s - 1)) + project(source(1, s - 1))
-
-    pl.semaphore_wait(entered.at[1], 2)
-    for to in along_x:
-        signal(entered.at[2], to)
-    relay(half - 1, True)
-    for s in (half - 2, half - 1):
-        acc[...] += project(source(0, s)) + project(source(1, s))
-    pl.semaphore_wait(entered.at[2], 2)
-    signal(entered.at[3], sibling)
+    both = [(d, j) for j in range(CHUNKS) for d in range(2)]
+    stops, ready = {}, {}
+    for d, j in both:
+        end = half if (j < CHUNKS // 2) == (d == 0) else half - 1
+        stops[d, j] = [0]
+        while stops[d, j][-1] < end:
+            t, at = len(stops[d, j]) - 1, stops[d, j][-1]
+            step = 2 if t % CHUNKS == j and at + 2 <= end else 1
+            for between in range(1, step + 1):
+                ready[d, at + between, j] = t + 1
+            stops[d, j].append(at + step)
+    hops = max(len(stop) for stop in stops.values()) - 1
+
+    pending = [(d, a) for a in range(half) for d in range(2 if a else 1)]
+    waited = set()
+
+    def need(d, a, j):
+        if (d, a, j) not in waited:
+            waited.add((d, a, j))
+            arrived(d, a, j)
+
+    def gathered(d, a):
+        for j in range(CHUNKS if a else 0):
+            need(d, a, j)
+
+    def project_one(t):
+        if pending:
+            d, a = pending[0]
+            if max([ready[d, a, j] for j in range(CHUNKS)] if a else [1]) <= t:
+                pending.pop(0)
+                gathered(d, a)
+                if a == 0:
+                    own.wait()
+                    weights.wait()
+                    acc[...] = project(z)
+                else:
+                    acc[...] += project(source(d, a))
+
+    def greet(t):
+        if t == 0:
+            for to in along_y:
+                signal(entered.at[0], to)
+        elif t == 2:
+            pl.semaphore_wait(entered.at[0], 2)
+            for to in along_x:
+                signal(entered.at[1], to)
+        elif t == hops - 2:
+            pl.semaphore_wait(entered.at[1], 2)
+            for to in along_x:
+                signal(entered.at[2], to)
+        elif t == hops - 1:
+            pl.semaphore_wait(entered.at[2], 2)
+            signal(entered.at[3], sibling)
+
+    for t in range(hops):
+        for group in range(2):
+            now = both[group * CHUNKS : (group + 1) * CHUNKS]
+            now = [(d, j) for d, j in now if t + 1 < len(stops[d, j])]
+            for d, j in now:
+                at, to = stops[d, j][t], stops[d, j][t + 1]
+                if t:
+                    need(d, at, j)
+                block = xbuf.at[source(d, at), part(j)] if t else x_ref.at[part(j)]
+                forward(d, at, to, j, block)
+            for d, j in now:
+                at, to = stops[d, j][t], stops[d, j][t + 1]
+                if to - at == 2:
+                    block = xbuf.at[source(d, at), part(j)] if t else x_ref.at[part(j)]
+                    forward(d, at, at + 1, j, block)
+            if t >= 3:
+                project_one(t - 1)
+        greet(t)
+    while pending:
+        project_one(hops)
     last = source(0, half)
-    for j in range(CHUNKS):
-        arrived(0 if j < CHUNKS // 2 else 1, half, j)
+    for d, j in both:
+        if stops[d, j][-1] == half:
+            need(d, half, j)
 
     def activated(begin, count):
         span = pl.ds(begin * HEAD, count * HEAD)

time: 102 us -> 101 us (level)
  Pallas kernels: 100 us -> 98.9 us
    pallas_call x1, Pallas kernels: 100 us -> 98.9 us  [body(): pl.pallas_call(functools.partial(kernel, nc, nx, nz, width), out_shape=ja...]
where the time goes in v3:
time: 101 us; the launch traced here: 100 us
  Pallas kernels  98.9 us (98%)
  local copies, waits for them, and re-layouts  1.57 us (2%)
    pallas_call x1, Pallas kernels, body(): pl.pallas_call(functools.partial(kernel, nc, nx, nz, width), out_shape=ja...  98.9 us

profile of v3, /device:TPU:1, one launch (start us, length us, event | category | flops | bytes accessed | tf_op | source)
XLA Modules:
  0.0 100.5 jit_solution(14870067337433329184)
XLA Ops:
  0.0 98.9 %shard_map.46 = bf16[256,256]{1,0:T(8,128)(2,1)} custom-call(bf16[192,256]{1,0:T(8,128)(2,1)} %x_ref.1, bf16[32,192,768]{2,1,0:T(8,128)(2,1)} %bitcast.2, f32[2,128,128]{2,1,0:T(8,128)} %prior_ref.1, f32[1,256]{1,0:T(1,128)} %bitcast.3), custom_call_target="tpu_custom_call" | custom-call | tf_op jit(solution)/shard_map/pallas_call | solution.py:305
  98.9 1.6 %copy.6 = bf16[256,256]{1,0:T(8,128)(2,1)} copy(bf16[256,256]{1,0:T(8,128)(2,1)} %shard_map.46) | data formatting | bytes 262144

commit v4 on v3

--- a/solution.py
+++ b/solution.py
@@ -162,7 +162,7 @@
                 if to - at == 2:
                     block = xbuf.at[source(d, at), part(j)] if t else x_ref.at[part(j)]
                     forward(d, at, at + 1, j, block)
-            if t >= 3:
+            for _ in range(group + 1 if t >= 2 else 0):
                 project_one(t - 1)
         greet(t)
     while pending:

time: 101 us -> 100 us (0.990)
  no operation moved by 1% of the time
where the time goes in v4:
time: 100 us; the launch traced here: 99.8 us
  Pallas kernels  98.2 us (98%)
  local copies, waits for them, and re-layouts  1.57 us (2%)
    pallas_call x1, Pallas kernels, body(): pl.pallas_call(functools.partial(kernel, nc, nx, nz, width), out_shape=ja...  98.2 us

profile of v4, /device:TPU:1, one launch (start us, length us, event | category | flops | bytes accessed | tf_op | source)
XLA Modules:
  0.0 99.8 jit_solution(840281742196732890)
XLA Ops:
  0.0 98.2 %shard_map.46 = bf16[256,256]{1,0:T(8,128)(2,1)} custom-call(bf16[192,256]{1,0:T(8,128)(2,1)} %x_ref.1, bf16[32,192,768]{2,1,0:T(8,128)(2,1)} %bitcast.2, f32[2,128,128]{2,1,0:T(8,128)} %prior_ref.1, f32[1,256]{1,0:T(1,128)} %bitcast.3), custom_call_target="tpu_custom_call" | custom-call | tf_op jit(solution)/shard_map/pallas_call | solution.py:305
  98.3 1.6 %copy.6 = bf16[256,256]{1,0:T(8,128)(2,1)} copy(bf16[256,256]{1,0:T(8,128)(2,1)} %shard_map.46) | data formatting | bytes 262144

commit v5 on v4

--- a/solution.py
+++ b/solution.py
@@ -162,7 +162,7 @@
                 if to - at == 2:
                     block = xbuf.at[source(d, at), part(j)] if t else x_ref.at[part(j)]
                     forward(d, at, at + 1, j, block)
-            for _ in range(group + 1 if t >= 2 else 0):
+            for _ in range(3 if group == 1 and t >= 2 else 0):
                 project_one(t - 1)
         greet(t)
     while pending:

time: 100 us -> 99.7 us (level)
  no operation moved by 1% of the time
where the time goes in v5:
time: 99.7 us; the launch traced here: 99.5 us
  Pallas kernels  97.9 us (98%)
  local copies, waits for them, and re-layouts  1.57 us (2%)
    pallas_call x1, Pallas kernels, body(): pl.pallas_call(functools.partial(kernel, nc, nx, nz, width), out_shape=ja...  97.9 us

profile of v5, /device:TPU:1, one launch (start us, length us, event | category | flops | bytes accessed | tf_op | source)
XLA Modules:
  0.0 99.5 jit_solution(7783404179198566886)
XLA Ops:
  0.0 97.9 %shard_map.46 = bf16[256,256]{1,0:T(8,128)(2,1)} custom-call(bf16[192,256]{1,0:T(8,128)(2,1)} %x_ref.1, bf16[32,192,768]{2,1,0:T(8,128)(2,1)} %bitcast.2, f32[2,128,128]{2,1,0:T(8,128)} %prior_ref.1, f32[1,256]{1,0:T(1,128)} %bitcast.3), custom_call_target="tpu_custom_call" | custom-call | tf_op jit(solution)/shard_map/pallas_call | solution.py:305
  98.0 1.6 %copy.6 = bf16[256,256]{1,0:T(8,128)(2,1)} copy(bf16[256,256]{1,0:T(8,128)(2,1)} %shard_map.46) | data formatting | bytes 262144
